TPU v7x, 512 devices: a whole 4x4x16 slice. The times are simulated.
512 devices in a mesh: dp: 4 (over x), expert: 128 (over z, y, core).
Axes of the slice: x: 4, y: 4, z: 16, core: 2. Of those that a mesh axis runs over, the one named last changes fastest.
Arguments:
- tokens: bfloat16 [65536, 2048], P(('dp', 'expert')), may hold values from -6 to 6
- hidden_grad: bfloat16 [65536, 1, 768], P(('dp', 'expert')), may hold values from -6 to 6
- gate_prob: float32 [65536, 1], P(('dp', 'expert')), may hold values from 0.2 to 1
- slot_choice: int32 [65536, 1], P(('dp', 'expert')), may hold values from 0 to 127; in each aligned block of 128 rows (0 to 127, 128 to 255, ...) at most 2 rows name the same one
- replica_plan: int32 [128], replicated, may hold values from 0 to 63, as said below
- weights: bfloat16 [64, 2, 2048, 768], P(None, None, ('dp', 'expert')), may hold values from -0.125 to 0.125
Outputs:
- input_grad: bfloat16 [65536, 2048], P(('dp', 'expert'))
- expert_grad: bfloat16 [64, 2, 2048, 768], P(None, None, ('dp', 'expert'))
Inputs may be any that keep to these rules, and one draw needn't show every extreme that they name: `slot_choice`: among the tokens of one device no slot is named more than 2 times, and 2 is reached; the picks of one token name different slots. `replica_plan`: every expert is held by at least one slot.
All inputs are finite; a program needn't handle non-finite values.
Results may differ from a plain program's by a relative error of at most 0.007.
Values may be sent and summed in bfloat16 or wider, within the bound.
A program may use at most 64 MiB of HBM per device.

v0:
```python
import jax
import jax.numpy as jnp
from jax import lax
from jax.sharding import PartitionSpec as P


def back_project(grad_gate, grad_up, weight_pair):
    contract_cols = (((1,), (1,)), ((), ()))
    first_term = lax.dot_general(
        grad_gate, weight_pair[0], contract_cols, preferred_element_type=jnp.float32
    )
    return first_term + lax.dot_general(
        grad_up, weight_pair[1], contract_cols, preferred_element_type=jnp.float32
    )


def row_products(inputs, grad_gate, grad_up):
    contract_rows = (((0,), (0,)), ((), ()))
    return jnp.stack(
        [
            lax.dot_general(inputs, grad_gate, contract_rows, preferred_element_type=jnp.float32),
            lax.dot_general(inputs, grad_up, contract_rows, preferred_element_type=jnp.float32),
        ]
    )


def per_device(tokens, hidden_grad, gate_prob, slot_choice, replica_plan, weights):
    expert_count = lax.axis_size("expert")
    group_count = lax.axis_size("dp")
    token_count, pick_count = slot_choice.shape
    row_count = token_count * pick_count
    capacity = max(2, 2 * row_count // expert_count)
    depth_rows = expert_count * capacity
    model_width = tokens.shape[1]
    hidden_width = hidden_grad.shape[2]
    expert_total = weights.shape[0]
    shard_rows = weights.shape[2]
    block_rows = shard_rows * expert_count
    flat_slot = slot_choice.reshape(row_count)
    slot_member = (flat_slot[:, None] == jnp.arange(expert_count, dtype=jnp.int32)[None, :]).astype(
        jnp.int32
    )
    ranking = jnp.sum((jnp.cumsum(slot_member, axis=0) - 1) * slot_member, axis=1)
    position = flat_slot * capacity + ranking
    scatter_table = (jnp.arange(depth_rows, dtype=jnp.int32)[:, None] == position[None, :]).astype(
        jnp.bfloat16
    )
    token_rows = jnp.repeat(tokens, pick_count, axis=0)
    cotangent = (gate_prob[:, :, None] * hidden_grad.astype(jnp.float32)).astype(jnp.bfloat16)
    cotangent = cotangent.reshape(row_count, hidden_width)
    send_inputs = jnp.dot(scatter_table, token_rows, preferred_element_type=jnp.float32).astype(
        jnp.bfloat16
    )
    send_cotangent = jnp.dot(scatter_table, cotangent, preferred_element_type=jnp.float32).astype(
        jnp.bfloat16
    )
    recv_inputs, recv_cotangent = (
        lax.all_to_all(
            send_inputs.reshape(expert_count, capacity, model_width),
            "expert",
            split_axis=0,
            concat_axis=0,
            tiled=True,
        ),
        lax.all_to_all(
            send_cotangent.reshape(expert_count, capacity, hidden_width),
            "expert",
            split_axis=0,
            concat_axis=0,
            tiled=True,
        ),
    )
    recv_inputs = recv_inputs.reshape(depth_rows, model_width)
    recv_cotangent = recv_cotangent.reshape(depth_rows, hidden_width)
    chooser = (replica_plan[:, None] == jnp.arange(expert_total, dtype=jnp.int32)[None, :]).astype(
        jnp.bfloat16
    )
    send_weights = jnp.einsum(
        "se,ekdf->skdf", chooser, weights, preferred_element_type=jnp.float32
    ).astype(jnp.bfloat16)
    own_weights = lax.all_to_all(
        send_weights, "expert", split_axis=0, concat_axis=2, tiled=True
    ).reshape(2, block_rows, hidden_width)
    piece = lax.all_gather(own_weights, "dp", axis=1, tiled=True)
    gate_sum = jnp.dot(recv_inputs, piece[0], preferred_element_type=jnp.float32)
    up_sum = jnp.dot(recv_inputs, piece[1], preferred_element_type=jnp.float32)
    sigma = jax.nn.sigmoid(gate_sum)
    scaled = recv_cotangent.astype(jnp.float32)
    grad_gate = (scaled * up_sum * sigma * (1.0 + gate_sum * (1.0 - sigma))).astype(jnp.bfloat16)
    grad_up = (scaled * gate_sum * sigma).astype(jnp.bfloat16)
    all_gate, all_up = (
        lax.all_gather(grad_gate, "dp", axis=0, tiled=True),
        lax.all_gather(grad_up, "dp", axis=0, tiled=True),
    )
    split_inputs = recv_inputs.reshape(depth_rows, group_count, block_rows)
    all_columns = lax.all_to_all(
        split_inputs, "dp", split_axis=1, concat_axis=0, tiled=True
    ).reshape(group_count * depth_rows, block_rows)
    row_terms = back_project(all_gate, all_up, own_weights).astype(jnp.bfloat16)
    summed = jnp.zeros((2, block_rows, hidden_width), jnp.float32)
    for group_index in range(group_count):
        lower = group_index * depth_rows
        upper = lower + depth_rows
        products = row_products(
            all_columns[lower:upper], all_gate[lower:upper], all_up[lower:upper]
        )
        summed = summed + lax.optimization_barrier(products.astype(jnp.bfloat16)).astype(
            jnp.float32
        )
    pieces = summed.reshape(2, expert_count, shard_rows, hidden_width)
    gathered = lax.all_to_all(
        pieces.astype(jnp.bfloat16), "expert", split_axis=1, concat_axis=1, tiled=True
    ).astype(pieces.dtype)
    membership = (
        jnp.arange(expert_total, dtype=jnp.int32)[:, None] == replica_plan[None, :]
    ).astype(jnp.float32)
    expert_grad = jnp.einsum("es,ksdf->ekdf", membership, gathered, precision=lax.Precision.HIGHEST)
    expert_grad = (expert_grad / group_count).astype(jnp.bfloat16)
    joined = lax.all_to_all(
        row_terms.reshape(group_count, depth_rows, block_rows),
        "dp",
        split_axis=0,
        concat_axis=2,
        tiled=True,
    )
    back_rows = lax.all_to_all(
        joined.reshape(expert_count, capacity, model_width),
        "expert",
        split_axis=0,
        concat_axis=0,
        tiled=True,
    )
    back_rows = back_rows.reshape(depth_rows, model_width)
    token_grads = lax.dot_general(
        scatter_table, back_rows, (((0,), (0,)), ((), ())), preferred_element_type=jnp.float32
    )
    input_grad = jnp.sum(token_grads.reshape(token_count, pick_count, model_width), axis=1).astype(
        jnp.bfloat16
    )
    return (input_grad, expert_grad)


def solution(mesh):
    placed = (
        P(("dp", "expert"), None),
        P(("dp", "expert"), None, None),
        P(("dp", "expert"), None),
        P(("dp", "expert"), None),
        P(),
        P(None, None, ("dp", "expert"), None),
    )
    return jax.shard_map(
        per_device,
        mesh=mesh,
        in_specs=placed,
        out_specs=(P(("dp", "expert"), None), P(None, None, ("dp", "expert"), None)),
        check_vma=False,
    )
```

profile of v0, /device:TPU:33, one launch (start us, length us, event | category | flops | bytes accessed | tf_op | source)
XLA Modules:
  0.0 494.8 jit_solution(11595988162404496423)
XLA Ops:
  7.2 1.1 copy-done
  8.3 1.3 convolution_convert_fusion.2
  9.6 1.2 copy.26
  10.8 96.8 %all_to_all.65 = bf16[128,2,4,768]{3,2,1,0:T(4,128)(2,1)S(1)} all-to-all(bf16[128,2,4,768]{3,2,1,0:T(4,128)(2,1)S(1)} %copy.26), channel_id=1, replica_groups=mesh['dp'=4,'expert'=128] {'expert'}, dimensions={0} | all-to-all | bytes 3145728 | tf_op jit(solution)/shard_map/all_to_all | solution.py:81
  107.6 2.4 copy.27
  110.0 0.6 copy-done.7
  111.4 0.9 reshape.66
  112.3 7.0 %all-to-all-start = ((bf16[128,2,768]{2,1,0:T(2,128)(2,1)}), bf16[128,2,768]{2,1,0:T(2,128)(2,1)S(1)}, u32[]{:S(2)}, u32[]{:S(2)}) async-start(bf16[128,2,768]{2,1,0:T(2,128)(2,1)} %reshape.66), calls=%async_computation | async-start | bytes 786432 | tf_op jit(solution)/shard_map/all_to_all | solution.py:65
  119.4 1.5 convolution_convert_fusion
  120.9 1.6 reshape.67
  122.5 25.1 %all-to-all-done = bf16[128,2,768]{2,1,0:T(2,128)(2,1)S(1)} async-done(((bf16[128,2,768]{2,1,0:T(2,128)(2,1)}), bf16[128,2,768]{2,1,0:T(2,128)(2,1)S(1)}, u32[]{:S(2)}, u32[]{:S(2)}) %all-to-all-start) | async-done | bytes 393248 | tf_op jit(solution)/shard_map/all_to_all | solution.py:65
  147.6 6.1 %all-to-all-start.1 = ((bf16[128,2,2048]{2,1,0:T(2,128)(2,1)}), bf16[128,2,2048]{2,1,0:T(2,128)(2,1)S(1)}, u32[]{:S(2)}, u32[]{:S(2)}) async-start(bf16[128,2,2048]{2,1,0:T(2,128)(2,1)} %reshape.67), calls=%async_computation.1 | async-start | bytes 2097152 | tf_op jit(solution)/shard_map/all_to_all | solution.py:58
  153.9 1.0 reshape.73
  154.9 54.4 %all-to-all-done.1 = bf16[128,2,2048]{2,1,0:T(2,128)(2,1)S(1)} async-done(((bf16[128,2,2048]{2,1,0:T(2,128)(2,1)}), bf16[128,2,2048]{2,1,0:T(2,128)(2,1)S(1)}, u32[]{:S(2)}, u32[]{:S(2)}) %all-to-all-start.1) | async-done | bytes 1048608 | tf_op jit(solution)/shard_map/all_to_all | solution.py:58
  209.3 1.3 reshape.68
  210.6 12.7 %fusion.40 = (bf16[1,2048,768]{2,0,1:T(2,128)(2,1)S(1)}, bf16[1,2048,768]{2,0,1:T(2,128)(2,1)S(1)}) fusion(bf16[2,2048,768]{2,0,1:T(2,128)(2,1)} %all-gather.4.cloned.1.call-done), kind=kLoop, calls=%fused_computation.69 | loop fusion | bytes 12582912 | tf_op jit(solution)/shard_map/slice | solution.py:85
  223.3 1.8 multiply_convert_fusion.1
  225.1 1.9 fusion.17
  227.1 0.7 all-gather.8.cloned.1.call-update
  227.8 1.4 fusion.41
  229.2 1.6 squeeze.15
  230.9 21.3 %all-gather.6.cloned.1.call-done = bf16[1024,768]{1,0:T(8,128)(2,1)} async-done(((bf16[256,768]{1,0:T(8,128)(2,1)}), bf16[1024,768]{1,0:T(8,128)(2,1)}) %all-gather.6.cloned.1.call-update) | async-done | bytes 1572880 | tf_op jit(solution)/shard_map/all_gather | solution.py:92
  252.3 3.8 fusion.42
  256.0 33.1 %all-gather.8.cloned.1.call-done = bf16[1024,768]{1,0:T(8,128)(2,1)} async-done(((bf16[256,768]{1,0:T(8,128)(2,1)}), bf16[1024,768]{1,0:T(8,128)(2,1)}) %all-gather.8.cloned.1.call-update) | async-done | bytes 1572880 | tf_op jit(solution)/shard_map/all_gather | solution.py:93
  289.1 4.1 add_convert_fusion.1
  293.2 3.5 all-to-all-start.3
  296.7 1.5 reshape_reshape.3
  298.2 2.4 copy.31
  300.6 10.4 %all-to-all-done.3 = bf16[4,256,512]{2,1,0:T(8,128)(2,1)S(1)} async-done(((bf16[4,256,512]{2,1,0:T(8,128)(2,1)}), bf16[4,256,512]{2,1,0:T(8,128)(2,1)S(1)}, u32[]{:S(2)}, u32[]{:S(2)}) %all-to-all-start.3) | async-done | bytes 1048608 | tf_op jit(solution)/shard_map/all_to_all | solution.py:119
  311.0 3.5 all-to-all-start.5
  314.6 1.8 copy.30
  316.3 2.3 reshape.71
  318.6 9.4 %all-to-all-done.5 = bf16[256,4,512]{2,0,1:T(8,128)(2,1)S(1)} async-done(((bf16[256,4,512]{2,0,1:T(8,128)(2,1)}), bf16[256,4,512]{2,0,1:T(8,128)(2,1)S(1)}, u32[]{:S(2)}, u32[]{:S(2)}) %all-to-all-start.5) | async-done | bytes 1048608 | tf_op jit(solution)/shard_map/all_to_all | solution.py:96
  328.0 18.6 %all-to-all-start.4 = ((bf16[128,2,2048]{2,1,0:T(2,128)(2,1)}), bf16[128,2,2048]{2,1,0:T(2,128)(2,1)S(1)}, u32[]{:S(2)}, u32[]{:S(2)}) async-start(bf16[128,2,2048]{2,1,0:T(2,128)(2,1)} %reshape.71), calls=%async_computation.4 | async-start | bytes 2097152 | tf_op jit(solution)/shard_map/all_to_all | solution.py:126
  346.6 1.4 fusion.12
  348.0 1.4 fusion.13
  349.6 1.2 copy-done.2
  351.9 0.4 fusion.6
  353.9 2.0 add_convert_fusion
  355.8 2.9 convert_element_type.82
  358.7 1.7 copy.32
  360.4 41.8 %all-to-all-done.4 = bf16[128,2,2048]{2,1,0:T(2,128)(2,1)S(1)} async-done(((bf16[128,2,2048]{2,1,0:T(2,128)(2,1)}), bf16[128,2,2048]{2,1,0:T(2,128)(2,1)S(1)}, u32[]{:S(2)}, u32[]{:S(2)}) %all-to-all-start.4) | async-done | bytes 1048608 | tf_op jit(solution)/shard_map/all_to_all | solution.py:126
  402.2 6.5 %all-to-all-start.6 = ((bf16[2,128,4,768]{3,2,0,1:T(4,128)(2,1)}), bf16[2,128,4,768]{3,2,0,1:T(4,128)(2,1)S(1)}, u32[]{:S(2)}, u32[]{:S(2)}) async-start(bf16[2,128,4,768]{3,2,0,1:T(4,128)(2,1)} %copy.32), calls=%async_computation.6 | async-start | bytes 3145728 | tf_op jit(solution)/shard_map/all_to_all | solution.py:111
  408.7 1.2 reshape.72
  410.0 2.4 convolution_convert_fusion.1
  412.4 73.8 %all-to-all-done.6 = bf16[2,128,4,768]{3,2,0,1:T(4,128)(2,1)S(1)} async-done(((bf16[2,128,4,768]{3,2,0,1:T(4,128)(2,1)}), bf16[2,128,4,768]{3,2,0,1:T(4,128)(2,1)S(1)}, u32[]{:S(2)}, u32[]{:S(2)}) %all-to-all-start.6) | async-done | bytes 1572896 | tf_op jit(solution)/shard_map/all_to_all | solution.py:111
  486.2 0.5 multiply_convert_fusion
  486.8 1.5 copy.34
  (38 shorter events, 4.0 us)
Async XLA Ops:
  7.2 1.1 copy-start
  7.2 203.4 %all-gather.4.cloned.1.call-start = ((), (), s32[]{:S(2)}) async-start(), calls=%async_computation.7 | async-start | bytes 7864320 | tf_op jit(solution)/shard_map/all_gather | solution.py:84
  110.0 0.7 copy-start.7
  110.0 1.1 copy-start.6
  110.0 1.1 copy-start.9
  112.3 35.2 %all-to-all-start = ((bf16[128,2,768]{2,1,0:T(2,128)(2,1)}), bf16[128,2,768]{2,1,0:T(2,128)(2,1)S(1)}, u32[]{:S(2)}, u32[]{:S(2)}) async-start(bf16[128,2,768]{2,1,0:T(2,128)(2,1)} %reshape.66), calls=%async_computation | async-start | bytes 786432 | tf_op jit(solution)/shard_map/all_to_all | solution.py:65
  147.6 61.7 %all-to-all-start.1 = ((bf16[128,2,2048]{2,1,0:T(2,128)(2,1)}), bf16[128,2,2048]{2,1,0:T(2,128)(2,1)S(1)}, u32[]{:S(2)}, u32[]{:S(2)}) async-start(bf16[128,2,2048]{2,1,0:T(2,128)(2,1)} %reshape.67), calls=%async_computation.1 | async-start | bytes 2097152 | tf_op jit(solution)/shard_map/all_to_all | solution.py:58
  153.7 98.6 %all-gather.6.cloned.1.call-start = ((), (), s32[]{:S(2)}) async-start(), calls=%async_computation.8 | async-start | bytes 1966080 | tf_op jit(solution)/shard_map/all_gather | solution.py:92
  210.6 12.7 %copy-start.5 = (f32[256,768]{1,0:T(8,128)S(1)}, f32[256,768]{1,0:T(8,128)}, u32[]{:S(2)}) copy-start(f32[256,768]{1,0:T(8,128)} %reshape.73) | copy-start | bytes 2359300
  210.6 12.7 %copy-start.4 = (bf16[256,2048]{1,0:T(8,128)(2,1)S(1)}, bf16[256,2048]{1,0:T(8,128)(2,1)}, u32[]{:S(2)}) copy-start(bf16[256,2048]{1,0:T(8,128)(2,1)} %reshape.68) | copy-start | bytes 3145732
  227.0 62.1 %all-gather.8.cloned.1.call-start = ((), (), s32[]{:S(2)}) async-start(), calls=%async_computation.9 | async-start | bytes 1966080 | tf_op jit(solution)/shard_map/all_gather | solution.py:93
  293.2 17.8 %all-to-all-start.3 = ((bf16[4,256,512]{2,1,0:T(8,128)(2,1)}), bf16[4,256,512]{2,1,0:T(8,128)(2,1)S(1)}, u32[]{:S(2)}, u32[]{:S(2)}) async-start(bf16[4,256,512]{2,1,0:T(8,128)(2,1)} %bitcast.99), calls=%async_computation.3 | async-start | bytes 2097152 | tf_op jit(solution)/shard_map/all_to_all | solution.py:119
  311.0 17.0 %all-to-all-start.5 = ((bf16[256,4,512]{2,0,1:T(8,128)(2,1)}), bf16[256,4,512]{2,0,1:T(8,128)(2,1)S(1)}, u32[]{:S(2)}, u32[]{:S(2)}) async-start(bf16[256,4,512]{2,0,1:T(8,128)(2,1)} %copy.31), calls=%async_computation.5 | async-start | bytes 2097152 | tf_op jit(solution)/shard_map/all_to_all | solution.py:96
  328.0 74.2 %all-to-all-start.4 = ((bf16[128,2,2048]{2,1,0:T(2,128)(2,1)}), bf16[128,2,2048]{2,1,0:T(2,128)(2,1)S(1)}, u32[]{:S(2)}, u32[]{:S(2)}) async-start(bf16[128,2,2048]{2,1,0:T(2,128)(2,1)} %reshape.71), calls=%async_computation.4 | async-start | bytes 2097152 | tf_op jit(solution)/shard_map/all_to_all | solution.py:126
  349.5 1.4 copy-start.2
  349.5 1.9 copy-start.3
  402.2 84.0 %all-to-all-start.6 = ((bf16[2,128,4,768]{3,2,0,1:T(4,128)(2,1)}), bf16[2,128,4,768]{3,2,0,1:T(4,128)(2,1)S(1)}, u32[]{:S(2)}, u32[]{:S(2)}) async-start(bf16[2,128,4,768]{3,2,0,1:T(4,128)(2,1)} %copy.32), calls=%async_computation.6 | async-start | bytes 3145728 | tf_op jit(solution)/shard_map/all_to_all | solution.py:111
  408.7 77.5 %copy-start.8 = (s32[128]{0:T(128)S(1)}, s32[128]{0:T(128)}, u32[]{:S(2)}) copy-start(s32[128]{0:T(128)} %param.10) | copy-start | bytes 1540
  410.0 78.3 %copy-start.1 = (bf16[64,2,4,768]{3,2,1,0:T(4,128)(2,1)S(1)}, bf16[64,2,4,768]{3,2,1,0:T(4,128)(2,1)}, u32[]{:S(2)}) copy-start(bf16[64,2,4,768]{3,2,1,0:T(4,128)(2,1)} %param.11) | copy-start | bytes 2359300
Sparse Core Ops, SparseCore 0:
  110.1 64.8 all-gather.3
  227.1 25.0 all-gather.5
  254.9 34.1 all-gather.7
where the time goes:
time: 496 us; the launch traced here: 495 us
  waiting for transfers between devices  270 us (54%)
  blocking collectives  96.8 us (20%)
  starting transfers between devices  45.6 us (9%)
  local copies, waits for them, and re-layouts  42.5 us (9%)
  matrix products  22.8 us (5%)
  between operations  14 us (3%)
    all_to_all x1, blocking collectives, per_device(): lax.all_to_all(send_weights, 'expert', split_axis=0, concat_axis=2, tiled...  96.8 us
    all_to_all x1, waiting for transfers between devices, per_device(): lax.all_to_all(pieces.astype(jnp.bfloat16), 'expert', split_axis=1, conca...  73.8 us
    all_to_all x1, waiting for transfers between devices, per_device(): lax.all_to_all(send_inputs.reshape(expert_count, capacity, model_width),...  54.4 us
    all_to_all x1, waiting for transfers between devices, per_device(): lax.all_to_all(joined.reshape(expert_count, capacity, model_width), 'expe...  41.8 us
    all_gather x1, waiting for transfers between devices, per_device(): lax.all_gather(grad_up, 'dp', axis=0, tiled=True)  33.1 us
    all_to_all x1, waiting for transfers between devices, per_device(): lax.all_to_all(send_cotangent.reshape(expert_count, capacity, hidden_widt...  25.1 us
    all_gather x1, waiting for transfers between devices, per_device(): lax.all_gather(grad_gate, 'dp', axis=0, tiled=True)  21.3 us
    all_to_all x1, starting transfers between devices, per_device(): lax.all_to_all(joined.reshape(expert_count, capacity, model_width), 'expe...  18.6 us
  transfers between devices with their start and end apart: 9, of which 8 were waited for; matrix products, arithmetic and copies ran while one was open for 8% of the time, Pallas kernels for 0%

commit v1 on v0

--- a/solution.py
+++ b/solution.py
@@ -90,7 +90,9 @@
     grad_up = (scaled * gate_sum * sigma).astype(jnp.bfloat16)
     all_gate, all_up = (
         lax.all_gather(grad_gate, "dp", axis=0, tiled=True),
-        lax.all_gather(grad_up, "dp", axis=0, tiled=True),
+        jnp.concatenate(
+            lax.all_to_all(jnp.stack([grad_up] * lax.axis_size("dp")), "dp", 0, 0), axis=0
+        ),
     )
     split_inputs = recv_inputs.reshape(depth_rows, group_count, block_rows)
     all_columns = lax.all_to_all(

time: 496 us -> 469 us (0.946)
  waiting for transfers between devices: 270 us -> 242 us
    all_gather x1 -> x0, waiting for transfers between devices: 33.1 us -> none  [per_device(): lax.all_gather(grad_up, 'dp', axis=0, tiled=True)]
    all_to_all x1, starting transfers between devices: 18.6 us -> 10.9 us  [per_device(): lax.all_to_all(joined.reshape(expert_count, capacity, model_width), 'expe...]
    all_gather x1, waiting for transfers between devices: 21.3 us -> 28.1 us  [per_device(): lax.all_gather(grad_gate, 'dp', axis=0, tiled=True)]
  transfers between devices with their start and end apart: 9 -> 9, of which waited for: 8 -> 7; matrix products, arithmetic and copies ran while one was open for 8% -> 9% of each run, Pallas kernels for 0% -> 0%
where the time goes in v1:
time: 469 us; the launch traced here: 468 us
  waiting for transfers between devices  242 us (52%)
  blocking collectives  96.8 us (21%)
  local copies, waits for them, and re-layouts  43.5 us (9%)
  starting transfers between devices  43 us (9%)
  matrix products  24.9 us (5%)
  between operations  14.3 us (3%)
    all_to_all x1, blocking collectives, per_device(): lax.all_to_all(send_weights, 'expert', split_axis=0, concat_axis=2, tiled...  96.8 us
    all_to_all x1, waiting for transfers between devices, per_device(): lax.all_to_all(pieces.astype(jnp.bfloat16), 'expert', split_axis=1, conca...  73.8 us
    all_to_all x1, waiting for transfers between devices, per_device(): lax.all_to_all(send_inputs.reshape(expert_count, capacity, model_width),...  54.4 us
    all_to_all x1, waiting for transfers between devices, per_device(): lax.all_to_all(joined.reshape(expert_count, capacity, model_width), 'expe...  40.9 us
    all_gather x1, waiting for transfers between devices, per_device(): lax.all_gather(grad_gate, 'dp', axis=0, tiled=True)  28.1 us
    all_to_all x1, waiting for transfers between devices, per_device(): lax.all_to_all(send_cotangent.reshape(expert_count, capacity, hidden_widt...  25.1 us
    slice x1, local copies, waits for them, and re-layouts, per_device(): piece[0]  12.7 us
    all_to_all x1, starting transfers between devices, per_device(): lax.all_to_all(joined.reshape(expert_count, capacity, model_width), 'expe...  10.9 us
  transfers between devices with their start and end apart: 9, of which 7 were waited for; matrix products, arithmetic and copies ran while one was open for 9% of the time, Pallas kernels for 0%

profile of v1, /device:TPU:33, one launch (start us, length us, event | category | flops | bytes accessed | tf_op | source)
XLA Modules:
  0.0 467.8 jit_solution(17639101478171728347)
XLA Ops:
  7.2 1.1 copy-done
  8.3 1.3 convolution_convert_fusion.2
  9.6 1.2 copy.26
  10.8 96.8 %all_to_all.70 = bf16[128,2,4,768]{3,2,1,0:T(4,128)(2,1)S(1)} all-to-all(bf16[128,2,4,768]{3,2,1,0:T(4,128)(2,1)S(1)} %copy.26), channel_id=1, replica_groups=mesh['dp'=4,'expert'=128] {'expert'}, dimensions={0} | all-to-all | bytes 3145728 | tf_op jit(solution)/shard_map/all_to_all | solution.py:81
  107.6 2.4 copy.27
  110.0 0.6 copy-done.6
  111.4 0.9 reshape.75
  112.3 7.0 %all-to-all-start = ((bf16[128,2,768]{2,1,0:T(2,128)(2,1)}), bf16[128,2,768]{2,1,0:T(2,128)(2,1)S(1)}, u32[]{:S(2)}, u32[]{:S(2)}) async-start(bf16[128,2,768]{2,1,0:T(2,128)(2,1)} %reshape.75), calls=%async_computation | async-start | bytes 786432 | tf_op jit(solution)/shard_map/all_to_all | solution.py:65
  119.4 1.5 convolution_convert_fusion
  120.9 1.6 reshape.76
  122.5 25.1 %all-to-all-done = bf16[128,2,768]{2,1,0:T(2,128)(2,1)S(1)} async-done(((bf16[128,2,768]{2,1,0:T(2,128)(2,1)}), bf16[128,2,768]{2,1,0:T(2,128)(2,1)S(1)}, u32[]{:S(2)}, u32[]{:S(2)}) %all-to-all-start) | async-done | bytes 393248 | tf_op jit(solution)/shard_map/all_to_all | solution.py:65
  147.6 6.1 %all-to-all-start.1 = ((bf16[128,2,2048]{2,1,0:T(2,128)(2,1)}), bf16[128,2,2048]{2,1,0:T(2,128)(2,1)S(1)}, u32[]{:S(2)}, u32[]{:S(2)}) async-start(bf16[128,2,2048]{2,1,0:T(2,128)(2,1)} %reshape.76), calls=%async_computation.1 | async-start | bytes 2097152 | tf_op jit(solution)/shard_map/all_to_all | solution.py:58
  153.9 1.0 reshape.83
  154.9 54.4 %all-to-all-done.1 = bf16[128,2,2048]{2,1,0:T(2,128)(2,1)S(1)} async-done(((bf16[128,2,2048]{2,1,0:T(2,128)(2,1)}), bf16[128,2,2048]{2,1,0:T(2,128)(2,1)S(1)}, u32[]{:S(2)}, u32[]{:S(2)}) %all-to-all-start.1) | async-done | bytes 1048608 | tf_op jit(solution)/shard_map/all_to_all | solution.py:58
  209.3 1.3 reshape.77
  210.5 12.7 %fusion.36 = (bf16[1,2048,768]{2,0,1:T(2,128)(2,1)S(1)}, bf16[1,2048,768]{2,0,1:T(2,128)(2,1)S(1)}) fusion(bf16[2,2048,768]{2,0,1:T(2,128)(2,1)} %all-gather.3.cloned.1.call-done), kind=kLoop, calls=%fused_computation.69 | loop fusion | bytes 12582912 | tf_op jit(solution)/shard_map/slice | solution.py:85
  223.3 1.8 multiply_convert_fusion.1
  225.1 1.9 fusion.17
  227.0 2.3 stack.55
  229.3 4.3 all-to-all-start.3
  233.6 1.4 fusion.37
  235.1 1.6 squeeze.15
  236.8 28.1 %all-gather.5.cloned.1.call-done = bf16[1024,768]{1,0:T(8,128)(2,1)} async-done(((bf16[256,768]{1,0:T(8,128)(2,1)}), bf16[1024,768]{1,0:T(8,128)(2,1)}) %all-gather.5.cloned.1.call-update) | async-done | bytes 1572880 | tf_op jit(solution)/shard_map/all_gather | solution.py:92
  264.9 3.7 fusion.38
  268.6 4.1 add_convert_fusion.1
  272.7 4.4 all-to-all-start.4
  277.1 1.5 reshape_reshape.3
  278.5 2.4 copy.31
  281.0 10.4 %all-to-all-done.4 = bf16[4,256,512]{2,1,0:T(8,128)(2,1)S(1)} async-done(((bf16[4,256,512]{2,1,0:T(8,128)(2,1)}), bf16[4,256,512]{2,1,0:T(8,128)(2,1)S(1)}, u32[]{:S(2)}, u32[]{:S(2)}) %all-to-all-start.4) | async-done | bytes 1048608 | tf_op jit(solution)/shard_map/all_to_all | solution.py:121
  291.4 3.5 all-to-all-start.6
  294.9 1.8 copy.30
  296.7 2.3 reshape.81
  299.0 9.4 %all-to-all-done.6 = bf16[256,4,512]{2,0,1:T(8,128)(2,1)S(1)} async-done(((bf16[256,4,512]{2,0,1:T(8,128)(2,1)}), bf16[256,4,512]{2,0,1:T(8,128)(2,1)S(1)}, u32[]{:S(2)}, u32[]{:S(2)}) %all-to-all-start.6) | async-done | bytes 1048608 | tf_op jit(solution)/shard_map/all_to_all | solution.py:98
  308.4 10.9 %all-to-all-start.5 = ((bf16[128,2,2048]{2,1,0:T(2,128)(2,1)}), bf16[128,2,2048]{2,1,0:T(2,128)(2,1)S(1)}, u32[]{:S(2)}, u32[]{:S(2)}) async-start(bf16[128,2,2048]{2,1,0:T(2,128)(2,1)} %reshape.81), calls=%async_computation.5 | async-start | bytes 2097152 | tf_op jit(solution)/shard_map/all_to_all | solution.py:128
  319.3 1.4 fusion.13
  320.7 1.4 fusion.11
  322.1 1.5 fusion.9
  323.7 1.4 fusion.7
  327.3 2.0 add_convert_fusion
  329.3 2.9 convert_element_type.82
  332.2 1.7 copy.32
  333.9 40.9 %all-to-all-done.5 = bf16[128,2,2048]{2,1,0:T(2,128)(2,1)S(1)} async-done(((bf16[128,2,2048]{2,1,0:T(2,128)(2,1)}), bf16[128,2,2048]{2,1,0:T(2,128)(2,1)S(1)}, u32[]{:S(2)}, u32[]{:S(2)}) %all-to-all-start.5) | async-done | bytes 1048608 | tf_op jit(solution)/shard_map/all_to_all | solution.py:128
  374.9 6.5 %all-to-all-start.7 = ((bf16[2,128,4,768]{3,2,0,1:T(4,128)(2,1)}), bf16[2,128,4,768]{3,2,0,1:T(4,128)(2,1)S(1)}, u32[]{:S(2)}, u32[]{:S(2)}) async-start(bf16[2,128,4,768]{3,2,0,1:T(4,128)(2,1)} %copy.32), calls=%async_computation.7 | async-start | bytes 3145728 | tf_op jit(solution)/shard_map/all_to_all | solution.py:113
  381.4 1.2 reshape.82
  382.6 2.4 convolution_convert_fusion.1
  385.1 73.8 %all-to-all-done.7 = bf16[2,128,4,768]{3,2,0,1:T(4,128)(2,1)S(1)} async-done(((bf16[2,128,4,768]{3,2,0,1:T(4,128)(2,1)}), bf16[2,128,4,768]{3,2,0,1:T(4,128)(2,1)S(1)}, u32[]{:S(2)}, u32[]{:S(2)}) %all-to-all-start.7) | async-done | bytes 1572896 | tf_op jit(solution)/shard_map/all_to_all | solution.py:113
  458.9 0.5 multiply_convert_fusion
  459.4 1.5 copy.34
  (36 shorter events, 3.5 us)
Async XLA Ops:
  7.2 1.1 copy-start
  7.2 203.4 %all-gather.3.cloned.1.call-start = ((), (), s32[]{:S(2)}) async-start(), calls=%async_computation.8 | async-start | bytes 7864320 | tf_op jit(solution)/shard_map/all_gather | solution.py:84
  110.0 0.7 copy-start.6
  110.0 1.1 copy-start.5
  110.0 1.1 copy-start.8
  112.3 35.2 %all-to-all-start = ((bf16[128,2,768]{2,1,0:T(2,128)(2,1)}), bf16[128,2,768]{2,1,0:T(2,128)(2,1)S(1)}, u32[]{:S(2)}, u32[]{:S(2)}) async-start(bf16[128,2,768]{2,1,0:T(2,128)(2,1)} %reshape.75), calls=%async_computation | async-start | bytes 786432 | tf_op jit(solution)/shard_map/all_to_all | solution.py:65
  147.6 61.7 %all-to-all-start.1 = ((bf16[128,2,2048]{2,1,0:T(2,128)(2,1)}), bf16[128,2,2048]{2,1,0:T(2,128)(2,1)S(1)}, u32[]{:S(2)}, u32[]{:S(2)}) async-start(bf16[128,2,2048]{2,1,0:T(2,128)(2,1)} %reshape.76), calls=%async_computation.1 | async-start | bytes 2097152 | tf_op jit(solution)/shard_map/all_to_all | solution.py:58
  153.7 111.2 %all-gather.5.cloned.1.call-start = ((), (), s32[]{:S(2)}) async-start(), calls=%async_computation.9 | async-start | bytes 1966080 | tf_op jit(solution)/shard_map/all_gather | solution.py:92
  210.5 12.8 %copy-start.4 = (f32[256,768]{1,0:T(8,128)S(1)}, f32[256,768]{1,0:T(8,128)}, u32[]{:S(2)}) copy-start(f32[256,768]{1,0:T(8,128)} %reshape.83) | copy-start | bytes 2359300
  210.5 12.8 %copy-start.3 = (bf16[256,2048]{1,0:T(8,128)(2,1)S(1)}, bf16[256,2048]{1,0:T(8,128)(2,1)}, u32[]{:S(2)}) copy-start(bf16[256,2048]{1,0:T(8,128)(2,1)} %reshape.77) | copy-start | bytes 3145732
  229.3 39.4 %all-to-all-start.3 = ((bf16[4,256,768]{2,1,0:T(8,128)(2,1)}), bf16[4,256,768]{2,1,0:T(8,128)(2,1)}, u32[]{:S(2)}, u32[]{:S(2)}) async-start(bf16[4,256,768]{2,1,0:T(8,128)(2,1)} %stack.55), calls=%async_computation.3 | async-start | bytes 3145728 | tf_op jit(solution)/shard_map/all_to_all | solution.py:94
  272.7 18.7 %all-to-all-start.4 = ((bf16[4,256,512]{2,1,0:T(8,128)(2,1)}), bf16[4,256,512]{2,1,0:T(8,128)(2,1)S(1)}, u32[]{:S(2)}, u32[]{:S(2)}) async-start(bf16[4,256,512]{2,1,0:T(8,128)(2,1)} %bitcast.112), calls=%async_computation.4 | async-start | bytes 2097152 | tf_op jit(solution)/shard_map/all_to_all | solution.py:121
  291.4 17.0 %all-to-all-start.6 = ((bf16[256,4,512]{2,0,1:T(8,128)(2,1)}), bf16[256,4,512]{2,0,1:T(8,128)(2,1)S(1)}, u32[]{:S(2)}, u32[]{:S(2)}) async-start(bf16[256,4,512]{2,0,1:T(8,128)(2,1)} %copy.31), calls=%async_computation.6 | async-start | bytes 2097152 | tf_op jit(solution)/shard_map/all_to_all | solution.py:98
  308.4 66.5 %all-to-all-start.5 = ((bf16[128,2,2048]{2,1,0:T(2,128)(2,1)}), bf16[128,2,2048]{2,1,0:T(2,128)(2,1)S(1)}, u32[]{:S(2)}, u32[]{:S(2)}) async-start(bf16[128,2,2048]{2,1,0:T(2,128)(2,1)} %reshape.81), calls=%async_computation.5 | async-start | bytes 2097152 | tf_op jit(solution)/shard_map/all_to_all | solution.py:128
  322.1 2.9 copy-start.2
  374.9 84.0 %all-to-all-start.7 = ((bf16[2,128,4,768]{3,2,0,1:T(4,128)(2,1)}), bf16[2,128,4,768]{3,2,0,1:T(4,128)(2,1)S(1)}, u32[]{:S(2)}, u32[]{:S(2)}) async-start(bf16[2,128,4,768]{3,2,0,1:T(4,128)(2,1)} %copy.32), calls=%async_computation.7 | async-start | bytes 3145728 | tf_op jit(solution)/shard_map/all_to_all | solution.py:113
  381.4 77.5 %copy-start.7 = (s32[128]{0:T(128)S(1)}, s32[128]{0:T(128)}, u32[]{:S(2)}) copy-start(s32[128]{0:T(128)} %param.10) | copy-start | bytes 1540
  382.6 78.3 %copy-start.1 = (bf16[64,2,4,768]{3,2,1,0:T(4,128)(2,1)S(1)}, bf16[64,2,4,768]{3,2,1,0:T(4,128)(2,1)}, u32[]{:S(2)}) copy-start(bf16[64,2,4,768]{3,2,1,0:T(4,128)(2,1)} %param.11) | copy-start | bytes 2359300
Sparse Core Ops, SparseCore 0:
  110.1 64.8 all-gather.2
  227.1 37.7 all-gather.4
